TPU v7x, 32 devices: a whole 2x2x4 slice. The times are simulated.
32 devices in a mesh: tm: 8 (over z, x), space: 4 (over y, core).
Axes of the slice: x: 2, y: 2, z: 4, core: 2. Of those that a mesh axis runs over, the one named last changes fastest.
Arguments:
- snapshots: float32 [4224, 4096], P('tm', 'space')
- starts: int32 [32], replicated, may hold values from 0 to 3968, as said below
- freq_lines: int32 [128], replicated, may hold values from 0 to 128, as said below
Outputs:
- power_density: float32 [128, 4096], P(None, ('space', 'tm'))
- gram_matrices: float32 [2, 128, 32, 32], P(None, 'tm')
Inputs may be any that keep to these rules, and one draw needn't show every extreme that they name: starts never fall, and block b starts at most 64 snapshots away from b * 128; the first block starts at 0 and the last at 3968. `freq_lines`: distinct line numbers in any order; 0 and 128 are among them.
All inputs are finite; a program needn't handle non-finite values.
Results may differ from a plain program's by a relative error of at most 0.0001.
Values sent between devices are 32-bit elements; how exact they have to be, the bound alone decides.
No kernel may reach another device: no remote copies, remote signals or barrier semaphores. Data moves between devices by JAX's collectives and lax.ppermute only.
A program may use at most 64 MiB of HBM per device.

v0:
```python
import math
import jax
import jax.numpy as jnp
from jax import lax
from jax.sharding import PartitionSpec as P

NFFT = 256
NF = 128
NB = 32


def spectral_table(freq_lines):
    moments = jnp.arange(NFFT, dtype=jnp.int32)
    cycle = freq_lines[:, None] * moments[None, :] % NFFT
    angles = 2.0 * math.pi / NFFT * cycle.astype(jnp.float32)
    window = 0.5 - 0.5 * jnp.cos(2.0 * math.pi / NFFT * moments.astype(jnp.float32))
    window = window / jnp.sqrt(jnp.sum(window * window))
    return jnp.concatenate(
        [window[None, :] * jnp.cos(angles), -window[None, :] * jnp.sin(angles)], axis=0
    )


def block_spectra(series, starts, table):
    offsets = starts[:, None] + jnp.arange(NFFT, dtype=jnp.int32)[None, :]
    blocks = series[offsets]
    return jnp.einsum("kt,btp->kbp", table, blocks, precision=lax.Precision.HIGHEST)


def local_terms(spectra, factor):
    highest = lax.Precision.HIGHEST
    real_part = spectra[:NF]
    imag_part = spectra[NF:]
    power = jnp.sum(real_part * real_part + imag_part * imag_part, axis=1) / NB
    gram_real = jnp.einsum("fbp,fcp->fbc", real_part, real_part, precision=highest) + jnp.einsum(
        "fbp,fcp->fbc", imag_part, imag_part, precision=highest
    )
    gram_imag = jnp.einsum("fbp,fcp->fbc", real_part, imag_part, precision=highest) - jnp.einsum(
        "fbp,fcp->fbc", imag_part, real_part, precision=highest
    )
    return (power, jnp.stack([gram_real, gram_imag]) * factor)


def body(snapshots, starts, freq_lines):
    groups = lax.axis_size("tm")
    columns = snapshots.shape[1] // groups
    table = spectral_table(freq_lines)
    arranged = snapshots.reshape(snapshots.shape[0], groups, columns)
    spectra = block_spectra(
        lax.all_to_all(arranged, "tm", split_axis=1, concat_axis=0, tiled=True)[:, 0, :],
        starts,
        table,
    )
    total_points = columns * groups * lax.axis_size("space")
    power_density, own_gram = local_terms(spectra, 1.0 / (NB * total_points))
    per_device = NF // groups
    summed = lax.psum(own_gram, ("tm", "space"))
    gram_matrices = lax.dynamic_slice_in_dim(
        summed, lax.axis_index("tm") * per_device, per_device, 1
    )
    return (power_density, gram_matrices)


def solution(mesh):
    placed = (P("tm", "space"), P(), P())
    return jax.shard_map(
        body,
        mesh=mesh,
        in_specs=placed,
        out_specs=(P(None, ("space", "tm")), P(None, "tm", None, None)),
        check_vma=False,
    )
```

profile of v0, /device:TPU:0, one launch (start us, length us, event | category | flops | bytes accessed | tf_op | source)
XLA Modules:
  0.0 276.6 jit_solution(2760193698736418181)
XLA Ops:
  7.2 0.0 copy-start
  7.2 1.6 copy-done
  8.8 1.5 copy_bitcast_fusion
  10.3 0.0 copy-start.2
  10.3 0.0 copy-start.3
  10.3 7.4 %all-to-all-start = ((f32[528,8,128]{2,0,1:T(8,128)}), f32[528,8,128]{2,0,1:T(8,128)}, u32[]{:S(2)}, u32[]{:S(2)}) async-start(f32[528,8,128]{2,0,1:T(8,128)} %copy_bitcast_fusion), calls=%async_computation | async-start | bytes 4325376 | tf_op jit(solution)/shard_map/all_to_all | solution.py:49
  17.7 0.0 all-reduce.2.cloned.1.call-start
  17.7 0.6 multiply_reduce_fusion
  19.1 0.0 copy-done.2
  19.1 0.1 fusion.25
  19.2 0.0 copy-done.3
  19.2 0.6 cosine_multiply_fusion
  19.9 47.6 %all-to-all-done = f32[528,8,128]{2,0,1:T(8,128)} async-done(((f32[528,8,128]{2,0,1:T(8,128)}), f32[528,8,128]{2,0,1:T(8,128)}, u32[]{:S(2)}, u32[]{:S(2)}) %all-to-all-start) | async-done | bytes 2162720 | tf_op jit(solution)/shard_map/all_to_all | solution.py:49
  67.4 29.4 %gather_fusion = f32[8192,128]{1,0:T(8,128)} fusion(f32[4224,128]{1,0:T(8,128)} %bitcast.3, s32[8192]{0:T(1024)S(1)} %broadcast_clamp_fusion), kind=kCustom, calls=%fused_computation | custom fusion | bytes 8421376 | tf_op jit(solution)/shard_map/gather | solution.py:25
  96.8 5.6 %fusion.16 = f32[256,32,128]{2,0,1:T(8,128)S(1)} fusion(f32[32,256,128]{2,1,0:T(8,128)} %bitcast.23, f32[128,256]{1,0:T(8,128)S(1)} %get-tuple-element.8, f32[128,256]{1,0:T(8,128)S(1)} %get-tuple-element.7), kind=kOutput, calls=%fused_computation.17 | convolution fusion | flops 3221291008 | bytes 8650752 | tf_op jit(solution)/shard_map/kt,btp->kbp/dot_general | solution.py:26
  102.4 0.7 fusion.29
  103.1 0.0 copy-start.1
  103.1 5.7 %fusion.4 = f32[128,32,32]{2,1,0:T(8,128)} fusion(f32[128,32,128]{2,0,1:T(8,128)S(1)} %get-tuple-element.6), kind=kOutput, calls=%fused_computation.9 | convolution fusion | flops 201326592 | bytes 2621440 | tf_op jit(solution)/shard_map/fbp,fcp->fbc/dot_general | solution.py:34
  108.8 5.7 %fusion = f32[128,32,32]{2,1,0:T(8,128)S(1)} fusion(f32[128,32,128]{2,0,1:T(8,128)S(1)} %get-tuple-element.6, f32[128,32,128]{2,0,1:T(8,128)S(1)} %get-tuple-element.4), kind=kOutput, calls=%fused_computation.5 | convolution fusion | flops 201326592 | bytes 4718592 | tf_op jit(solution)/shard_map/fbp,fcp->fbc/dot_general | solution.py:37
  114.5 0.0 copy-done.1
  114.5 7.2 %subtract_bitcast_fusion = f32[1,128,32,32]{3,2,1,0:T(8,128)} fusion(f32[128,32,32]{2,1,0:T(8,128)S(1)} %fusion, f32[128,32,128]{2,0,1:T(8,128)S(1)} %get-tuple-element.6, f32[128,32,128]{2,0,1:T(8,128)S(1)} %get-tuple-element.4), kind=kOutput, calls=%fused_computation.2 | convolution fusion | flops 201457664 | bytes 5242880 | tf_op jit(solution)/shard_map/fbp,fcp->fbc/dot_general | solution.py:37
  121.7 2.7 copy.33
  124.3 9.7 %add_bitcast_fusion = f32[1,128,32,32]{3,2,1,0:T(8,128)} fusion(f32[128,32,32]{2,1,0:T(8,128)} %fusion.4, f32[128,32,128]{2,0,1:T(8,128)} %copy-done.1), kind=kOutput, calls=%fused_computation.3 | convolution fusion | flops 201457664 | bytes 3145728 | tf_op jit(solution)/shard_map/fbp,fcp->fbc/dot_general | solution.py:34
  134.1 2.7 copy.32
  136.7 1.1 maximum_multiply_fusion
  137.8 0.0 all-reduce.2.cloned.1.call-update
  137.9 0.6 broadcast_multiply_fusion
  138.5 128.4 %all-reduce.2.cloned.1.call-done = f32[2,128,32,32]{1,3,2,0:T(8,128)} async-done(((f32[2,128,32,32]{1,3,2,0:T(8,128)}), f32[2,128,32,32]{1,3,2,0:T(8,128)}) %all-reduce.2.cloned.1.call-update) | async-done | bytes 1048592 | tf_op jit(solution)/shard_map/psum | solution.py:56
  266.9 1.6 constant_dynamic-slice_fusion
  268.5 1.2 copy.34
  (3 shorter events, 0.1 us)
Async XLA Ops:
  7.2 1.6 copy-start
  10.3 8.8 %copy-start.2 = (s32[32]{0:T(128)S(1)}, s32[32]{0:T(128)}, u32[]{:S(2)}) copy-start(s32[32]{0:T(128)} %param.4) | copy-start | bytes 388
  10.3 9.0 %copy-start.3 = (s32[128]{0:T(128)S(1)}, s32[128]{0:T(128)}, u32[]{:S(2)}) copy-start(s32[128]{0:T(128)} %param.5) | copy-start | bytes 1540
  10.3 57.1 %all-to-all-start = ((f32[528,8,128]{2,0,1:T(8,128)}), f32[528,8,128]{2,0,1:T(8,128)}, u32[]{:S(2)}, u32[]{:S(2)}) async-start(f32[528,8,128]{2,0,1:T(8,128)} %copy_bitcast_fusion), calls=%async_computation | async-start | bytes 4325376 | tf_op jit(solution)/shard_map/all_to_all | solution.py:49
  17.7 249.3 %all-reduce.2.cloned.1.call-start = ((), (), s32[]{:S(2)}) async-start(), calls=%async_computation.1 | async-start | bytes 2097152 | tf_op jit(solution)/shard_map/psum | solution.py:56
  103.1 11.4 %copy-start.1 = (f32[128,32,128]{2,0,1:T(8,128)}, f32[128,32,128]{2,0,1:T(8,128)S(1)}, u32[]{:S(2)}) copy-start(f32[128,32,128]{2,0,1:T(8,128)S(1)} %get-tuple-element.4) | copy-start | bytes 6291460
Sparse Core Ops, SparseCore 0:
  138.0 128.9 all-reduce.1
where the time goes:
time: 277 us
  waiting for transfers between devices  176 us (64%)
  local copies, waits for them, and re-layouts  40.6 us (15%)
  matrix products  33.9 us (12%)
  between operations  14.8 us (5%)
  starting transfers between devices  7.42 us (3%)
  other arithmetic  3.87 us (1%)
    psum x1, waiting for transfers between devices, body(): summed = lax.psum(own_gram, ('tm', 'space'))  128 us
    all_to_all x1, waiting for transfers between devices, body(): lax.all_to_all(arranged, 'tm', split_axis=1, concat_axis=0, tiled=True)  47.6 us
    gather x1, local copies, waits for them, and re-layouts, block_spectra(): blocks = series[offsets]  29.4 us
    dot_general x1, matrix products, local_terms(): jnp.einsum('fbp,fcp->fbc', real_part, real_part, precision=highest)  9.72 us
    all_to_all x1, starting transfers between devices, body(): lax.all_to_all(arranged, 'tm', split_axis=1, concat_axis=0, tiled=True)  7.38 us
    dot_general x1, matrix products, local_terms(): jnp.einsum('fbp,fcp->fbc', real_part, imag_part, precision=highest)  7.21 us
    dot_general x1, matrix products, local_terms(): jnp.einsum('fbp,fcp->fbc', imag_part, imag_part, precision=highest)  5.68 us
    dot_general x1, matrix products, local_terms(): jnp.einsum('fbp,fcp->fbc', imag_part, real_part, precision=highest)  5.67 us
  transfers between devices with their start and end apart: 2, of which 2 were waited for; matrix products, arithmetic and copies ran while one was open for 1% of the time, Pallas kernels for 0%

commit v1 on v0

--- a/solution.py
+++ b/solution.py
@@ -53,7 +53,8 @@
     total_points = columns * groups * lax.axis_size("space")
     power_density, own_gram = local_terms(spectra, 1.0 / (NB * total_points))
     per_device = NF // groups
-    summed = lax.psum(own_gram, ("tm", "space"))
+    shards = lax.all_gather(own_gram, ("tm", "space"), axis=0, tiled=False)
+    summed = shards.sum(axis=0)
     gram_matrices = lax.dynamic_slice_in_dim(
         summed, lax.axis_index("tm") * per_device, per_device, 1
     )

time: 277 us -> 355 us (1.28)
  waiting for transfers between devices: 176 us -> 241 us
  other arithmetic: 3.87 us -> 16.1 us
    all_gather x0 -> x1, waiting for transfers between devices: none -> 193 us  [body(): shards = lax.all_gather(own_gram, ('tm', 'space'), axis=0, tiled=False)]
    psum x1 -> x0, waiting for transfers between devices: 128 us -> none  [body(): summed = lax.psum(own_gram, ('tm', 'space'))]
    reduce_sum x0 -> x1, other arithmetic: none -> 12.3 us  [body(): summed = shards.sum(axis=0)]
where the time goes in v1:
time: 355 us
  waiting for transfers between devices  241 us (68%)
  local copies, waits for them, and re-layouts  41.5 us (12%)
  matrix products  33.9 us (10%)
  other arithmetic  16.1 us (5%)
  between operations  14.8 us (4%)
  starting transfers between devices  7.42 us (2%)
    all_gather x1, waiting for transfers between devices, body(): shards = lax.all_gather(own_gram, ('tm', 'space'), axis=0, tiled=False)  193 us
    all_to_all x1, waiting for transfers between devices, body(): lax.all_to_all(arranged, 'tm', split_axis=1, concat_axis=0, tiled=True)  47.6 us
    gather x1, local copies, waits for them, and re-layouts, block_spectra(): blocks = series[offsets]  29.4 us
    reduce_sum x1, other arithmetic, body(): summed = shards.sum(axis=0)  12.3 us
    dot_general x1, matrix products, local_terms(): jnp.einsum('fbp,fcp->fbc', real_part, real_part, precision=highest)  9.72 us
    all_to_all x1, starting transfers between devices, body(): lax.all_to_all(arranged, 'tm', split_axis=1, concat_axis=0, tiled=True)  7.38 us
    dot_general x1, matrix products, local_terms(): jnp.einsum('fbp,fcp->fbc', real_part, imag_part, precision=highest)  7.21 us
  transfers between devices with their start and end apart: 2, of which 2 were waited for; matrix products, arithmetic and copies ran while one was open for 1% of the time, Pallas kernels for 0%

profile of v1, /device:TPU:0, one launch (start us, length us, event | category | flops | bytes accessed | tf_op | source)
XLA Modules:
  0.0 354.7 jit_solution(14057747708172758820)
XLA Ops:
  7.2 0.0 copy-start
  7.2 1.6 copy-done
  8.8 1.5 copy_bitcast_fusion
  10.3 0.0 copy-start.2
  10.3 0.0 copy-start.3
  10.3 7.4 %all-to-all-start = ((f32[528,8,128]{2,0,1:T(8,128)}), f32[528,8,128]{2,0,1:T(8,128)}, u32[]{:S(2)}, u32[]{:S(2)}) async-start(f32[528,8,128]{2,0,1:T(8,128)} %copy_bitcast_fusion), calls=%async_computation | async-start | bytes 4325376 | tf_op jit(solution)/shard_map/all_to_all | solution.py:49
  17.7 0.0 all-gather.2.cloned.1.call-start
  17.7 0.0 copy-done.2
  17.7 0.1 fusion.25
  17.8 0.6 multiply_reduce_fusion
  19.2 0.0 copy-done.3
  19.2 0.6 cosine_multiply_fusion
  19.9 47.6 %all-to-all-done = f32[528,8,128]{2,0,1:T(8,128)} async-done(((f32[528,8,128]{2,0,1:T(8,128)}), f32[528,8,128]{2,0,1:T(8,128)}, u32[]{:S(2)}, u32[]{:S(2)}) %all-to-all-start) | async-done | bytes 2162720 | tf_op jit(solution)/shard_map/all_to_all | solution.py:49
  67.4 29.4 %gather_fusion = f32[8192,128]{1,0:T(8,128)} fusion(f32[4224,128]{1,0:T(8,128)} %bitcast.3, s32[8192]{0:T(1024)S(1)} %broadcast_clamp_fusion), kind=kCustom, calls=%fused_computation | custom fusion | bytes 8421376 | tf_op jit(solution)/shard_map/gather | solution.py:25
  96.8 5.6 %fusion.16 = f32[256,32,128]{2,0,1:T(8,128)S(1)} fusion(f32[32,256,128]{2,1,0:T(8,128)} %bitcast.23, f32[128,256]{1,0:T(8,128)S(1)} %get-tuple-element.8, f32[128,256]{1,0:T(8,128)S(1)} %get-tuple-element.7), kind=kOutput, calls=%fused_computation.17 | convolution fusion | flops 3221291008 | bytes 8650752 | tf_op jit(solution)/shard_map/kt,btp->kbp/dot_general | solution.py:26
  102.4 0.7 fusion.29
  103.1 0.0 copy-start.1
  103.1 5.7 %fusion.4 = f32[128,32,32]{2,1,0:T(8,128)} fusion(f32[128,32,128]{2,0,1:T(8,128)S(1)} %get-tuple-element.6), kind=kOutput, calls=%fused_computation.9 | convolution fusion | flops 201326592 | bytes 2621440 | tf_op jit(solution)/shard_map/fbp,fcp->fbc/dot_general | solution.py:34
  108.8 5.7 %fusion = f32[128,32,32]{2,1,0:T(8,128)S(1)} fusion(f32[128,32,128]{2,0,1:T(8,128)S(1)} %get-tuple-element.6, f32[128,32,128]{2,0,1:T(8,128)S(1)} %get-tuple-element.4), kind=kOutput, calls=%fused_computation.5 | convolution fusion | flops 201326592 | bytes 4718592 | tf_op jit(solution)/shard_map/fbp,fcp->fbc/dot_general | solution.py:37
  114.5 0.0 copy-done.1
  114.5 7.2 %subtract_bitcast_fusion = f32[1,1,128,32,32]{4,3,2,1,0:T(8,128)} fusion(f32[128,32,32]{2,1,0:T(8,128)S(1)} %fusion, f32[128,32,128]{2,0,1:T(8,128)S(1)} %get-tuple-element.6, f32[128,32,128]{2,0,1:T(8,128)S(1)} %get-tuple-element.4), kind=kOutput, calls=%fused_computation.2 | convolution fusion | flops 201457664 | bytes 5242880 | tf_op jit(solution)/shard_map/fbp,fcp->fbc/dot_general | solution.py:37
  121.7 2.7 copy.44
  124.3 9.7 %add_bitcast_fusion = f32[1,1,128,32,32]{4,3,2,1,0:T(8,128)} fusion(f32[128,32,32]{2,1,0:T(8,128)} %fusion.4, f32[128,32,128]{2,0,1:T(8,128)} %copy-done.1), kind=kOutput, calls=%fused_computation.3 | convolution fusion | flops 201457664 | bytes 3145728 | tf_op jit(solution)/shard_map/fbp,fcp->fbc/dot_general | solution.py:34
  134.1 2.7 copy.43
  136.7 1.1 maximum_multiply_fusion
  137.8 0.0 all-gather.2.cloned.1.call-update
  137.8 0.6 broadcast_multiply_fusion
  138.5 193.4 %all-gather.2.cloned.1.call-done = f32[32,2,128,32,32]{2,4,3,1,0:T(8,128)} async-done(((f32[1,2,128,32,32]{2,4,3,1,0:T(8,128)}), f32[32,2,128,32,32]{2,4,3,1,0:T(8,128)}) %all-gather.2.cloned.1.call-update) | async-done | bytes 33554448 | tf_op jit(solution)/shard_map/all_gather | solution.py:56
  331.9 12.3 %reduce_sum.29 = f32[2,128,32,32]{1,3,2,0:T(8,128)S(1)} reduce(f32[32,2,128,32,32]{2,4,3,1,0:T(8,128)} %all-gather.2.cloned.1.call-done, f32[]{:T(128)} %constant.15.clone.1), dimensions={0}, to_apply=%region_2.3 | reduce | flops 8126464 | bytes 34603012 | tf_op jit(solution)/shard_map/reduce_sum | solution.py:57
  344.1 1.3 constant_dynamic-slice_fusion
  345.5 2.4 copy.45
  (3 shorter events, 0.1 us)
Async XLA Ops:
  7.2 1.6 copy-start
  10.3 7.4 %copy-start.2 = (s32[32]{0:T(128)S(1)}, s32[32]{0:T(128)}, u32[]{:S(2)}) copy-start(s32[32]{0:T(128)} %param.4) | copy-start | bytes 388
  10.3 8.9 %copy-start.3 = (s32[128]{0:T(128)S(1)}, s32[128]{0:T(128)}, u32[]{:S(2)}) copy-start(s32[128]{0:T(128)} %param.5) | copy-start | bytes 1540
  10.3 57.1 %all-to-all-start = ((f32[528,8,128]{2,0,1:T(8,128)}), f32[528,8,128]{2,0,1:T(8,128)}, u32[]{:S(2)}, u32[]{:S(2)}) async-start(f32[528,8,128]{2,0,1:T(8,128)} %copy_bitcast_fusion), calls=%async_computation | async-start | bytes 4325376 | tf_op jit(solution)/shard_map/all_to_all | solution.py:49
  17.7 314.2 %all-gather.2.cloned.1.call-start = ((), (), s32[]{:S(2)}) async-start(), calls=%async_computation.1 | async-start | bytes 34603008 | tf_op jit(solution)/shard_map/all_gather | solution.py:56
  103.1 11.4 %copy-start.1 = (f32[128,32,128]{2,0,1:T(8,128)}, f32[128,32,128]{2,0,1:T(8,128)S(1)}, u32[]{:S(2)}) copy-start(f32[128,32,128]{2,0,1:T(8,128)S(1)} %get-tuple-element.4) | copy-start | bytes 6291460
Sparse Core Ops, SparseCore 0:
  137.9 193.8 all-gather.1
